TPU v7x, 32 devices: a whole 2x2x4 slice. The times are simulated.
32 devices in a mesh: group: 2 (over y), swap: 8 (over z, x), image: 2 (over core).
Axes of the slice: x: 2, y: 2, z: 4, core: 2. Of those that a mesh axis runs over, the one named last changes fastest.
Arguments:
- images_in: bfloat16 [16, 1536, 4096], P(('group', 'image'), 'swap'), parts along dimension 0, may hold values from -6 to 6
- kernel: bfloat16 [1536, 49], P('swap'), may hold values from -1.75 to 1.75
- conv_bias: float32 [1536], P('swap'), may hold values from -1 to 1
- norm_gain: float32 [1536], replicated, may hold values from 0.1 to 1.9
- norm_shift: float32 [1536], replicated, may hold values from -0.5 to 0.5
- fp8_weight: bfloat16 [1536, 6144], P('swap', 'image'), may hold values from -1.875 to 1.875, as said below
- block_scale: int32 [1536, 48], P('swap', 'image'), may hold values from -7 to -5
- adapter_a: bfloat16 [1536, 32], replicated, may hold values from -0.15625 to 0.15625
- adapter_b: bfloat16 [32, 6144], P(None, 'image'), may hold values from -0.25 to 0.25
- cotangent: bfloat16 [16, 4096, 6144], P('group', 'swap', 'image'), parts along dimension 0, may hold values from -0.05 to 0.05
Outputs:
- grad_a: float32 [3072, 32], P('group'), parts along dimension 0
- grad_b: float32 [64, 6144], P('group', 'image'), parts along dimension 0
There are 2 independent parts, one for each index of `group`. A program takes and returns all parts, laid end to end along the dimension named above; an argument that names none is the same for every part. Nothing has to cross between parts.
Inputs may be any that keep to these rules, and one draw needn't show every extreme that they name: `fp8_weight`: each entry is a value of the E4M3 format: a sign times 2 to an integer power times 1 + k / 8 for an integer k of 0 to 7. `block_scale`: the entry at [c, j] is the exponent of the scale of hidden units 128 * j to 128 * j + 127 of weight row c.
All inputs are finite; a program needn't handle non-finite values.
Results may differ from a plain program's by a relative error of at most 0.00055.
The roundings to bfloat16 on the way count: a program that leaves them out, or rounds other values in their place, can miss the bound.
Values may be sent and summed in bfloat16 or wider, within the bound.
A program may use at most 192 MiB of HBM per device.

v0:
```python
import jax
import jax.numpy as jnp
from jax import lax
from jax.sharding import PartitionSpec as P

KS = 7
W = 64
adapter_scale = 2.0
norm_eps = 1e-06


def power_table(scales):
    factor = jnp.zeros(scales.shape, jnp.float32)
    for exponent in range(-12, 4):
        factor = factor + jnp.where(
            scales == exponent, jnp.float32(2.0**exponent), jnp.float32(0.0)
        )
    return factor


def decode(weight, scales):
    row_count = weight.shape[0]
    groups = scales.shape[1]
    blocks = (
        weight.reshape(row_count, groups, -1).astype(jnp.float32) * power_table(scales)[:, :, None]
    )
    return blocks.reshape(row_count, -1).astype(jnp.bfloat16)


def gelu_slope(pre_act):
    cumulative = 0.5 * (1.0 + jax.scipy.special.erf(pre_act * 0.7071067811865476))
    density = jnp.exp(-0.5 * pre_act * pre_act) * 0.3989422804014327
    return cumulative + pre_act * density


def depthwise(images, kernel, conv_bias, map_width):
    batch, channels, pixels = images.shape
    maps = images.reshape(batch, channels, pixels // map_width, map_width)
    taps = kernel.reshape(channels, 1, KS, KS)
    half_span = KS // 2
    summed = lax.conv_general_dilated(
        maps,
        taps,
        (1, 1),
        ((half_span, half_span), (half_span, half_span)),
        dimension_numbers=("NCHW", "OIHW", "NCHW"),
        feature_group_count=channels,
        preferred_element_type=jnp.float32,
    )
    summed = summed.reshape(batch, channels, pixels)
    return summed + conv_bias[None, :, None]


def shards(
    images_in,
    kernel,
    conv_bias,
    norm_gain,
    norm_shift,
    fp8_weight,
    block_scale,
    adapter_a,
    adapter_b,
    cotangent,
):
    conv = depthwise(images_in, kernel, conv_bias, W).astype(jnp.bfloat16)
    values = lax.all_to_all(conv, "swap", split_axis=2, concat_axis=1, tiled=True).astype(
        jnp.float32
    )
    average = jnp.mean(values, axis=1, keepdims=True)
    centred = values - average
    variance = jnp.mean(centred * centred, axis=1, keepdims=True)
    scaled = (
        centred * lax.rsqrt(variance + norm_eps) * norm_gain[None, :, None]
        + norm_shift[None, :, None]
    )
    normed = jnp.swapaxes(scaled, 1, 2).astype(jnp.bfloat16)
    own_rows = normed.reshape(-1, normed.shape[2])
    tokens = lax.all_gather(own_rows, "image", axis=0, tiled=True)
    zero_start = jnp.zeros((tokens.shape[0], fp8_weight.shape[1]), jnp.float32)
    local_weight = decode(fp8_weight, block_scale)
    shard_rows = lax.all_gather(local_weight, "swap", axis=0, tiled=True)
    columns = lax.slice_in_dim(tokens, 0, shard_rows.shape[0], axis=1)
    frozen = zero_start + jnp.dot(columns, shard_rows, preferred_element_type=jnp.float32)
    low_rank = jnp.dot(tokens, adapter_a, preferred_element_type=jnp.float32).astype(jnp.bfloat16)
    pre_act = frozen + adapter_scale * jnp.dot(
        low_rank, adapter_b, preferred_element_type=jnp.float32
    )
    upstream = cotangent.reshape(-1, cotangent.shape[2])
    grad_pre = (upstream.astype(jnp.float32) * gelu_slope(pre_act)).astype(jnp.bfloat16)
    grad_b_local = adapter_scale * jnp.dot(low_rank.T, grad_pre, preferred_element_type=jnp.float32)
    partial_back = jnp.dot(grad_pre, adapter_b.T, preferred_element_type=jnp.float32)
    contract = (((0,), (0,)), ((), ()))
    tokens_wide = tokens.astype(jnp.float32)
    summed_back = lax.psum(partial_back, "image")
    grad_a_local = adapter_scale * lax.dot_general(
        tokens_wide,
        summed_back,
        contract,
        precision=lax.Precision.HIGHEST,
        preferred_element_type=jnp.float32,
    )
    grad_a, grad_b = lax.psum((grad_a_local, grad_b_local), "swap")
    return (grad_a, grad_b)


def solution(mesh):
    placed = (
        P(("group", "image"), "swap", None),
        P("swap", None),
        P("swap"),
        P(),
        P(),
        P("swap", "image"),
        P("swap", "image"),
        P(),
        P(None, "image"),
        P("group", "swap", "image"),
    )
    return jax.shard_map(
        shards,
        mesh=mesh,
        in_specs=placed,
        out_specs=(P("group", None), P("group", "image")),
        check_vma=False,
    )
```

profile of v0, /device:TPU:0, one launch (start us, length us, event | category | flops | bytes accessed | tf_op | source)
XLA Modules:
  0.0 837.5 jit_solution(14557225846373415734)
XLA Ops:
  7.2 0.0 copy-start
  7.2 0.0 all-gather.3.cloned.1.call-start
  7.2 0.8 reshape.62
  8.1 10.6 %copy.43 = bf16[4,192,4096]{1,2,0:T(8,128)(2,1)} copy(bf16[4,192,4096]{2,1,0:T(8,128)(2,1)} %param.10) | data formatting | bytes 12582912 | tf_op args[0]
  18.7 11.5 %copy.54 = bf16[192,64,4,64]{0,1,3,2:T(8,128)(2,1)} copy(bf16[192,64,4,64]{0,3,1,2:T(8,128)(2,1)} %bitcast.75) | data formatting | bytes 12582912
  30.2 10.0 %pad.clone = bf16[192,64,4,72]{0,1,3,2:T(8,128)(2,1)} pad(bf16[192,64,4,64]{0,1,3,2:T(8,128)(2,1)} %copy.54, bf16[]{:T(256)} %constant.37), padding=0_0x0_0x0_0x3_5 | pad | bytes 13369346 | tf_op jit(solution)/shard_map/reshape | solution.py:38
  40.2 3.4 slice.2
  43.7 1.9 copy-done.2
  45.5 4.2 fusion.8
  49.7 95.5 %broadcast_select_fusion = f32[64,32,9,192]{3,1,2,0:T(8,128)S(1)} fusion(pred[32,9]{0,1:T(8,128)(4,1)S(1)} %copy-done.9, bf16[192,1,7,7]{0,1,3,2:T(2,128)(2,1)S(1)} %reshape.62, bf16[192,64,4,8,15]{0,1,4,3,2:T(8,128)(2,1)S(1)} %fusion.8), kind=kOutput, calls=%fused_computation.23 | convolution fusion | flops 341065728 | bytes 25971360 | tf_op jit(solution)/shard_map/conv_general_dilated | solution.py:41
  145.3 20.1 %copy.47 = f32[64,32,9,192]{3,0,2,1:T(8,128)S(1)} copy(f32[64,32,9,192]{3,1,2,0:T(8,128)S(1)} %broadcast_select_fusion) | data formatting | bytes 28311552 | tf_op jit(solution)/shard_map/conv_general_dilated | solution.py:41
  165.4 2.0 slice_bitcast_fusion
  167.4 0.0 copy-start.8
  167.4 17.9 %copy.48 = f32[4,192,64,64]{1,3,2,0:T(8,128)S(1)} copy(f32[4,192,64,64]{1,2,3,0:T(8,128)S(1)} %slice_bitcast_fusion) | data formatting | bytes 25165824 | tf_op jit(solution)/shard_map/conv_general_dilated | solution.py:41
  185.3 2.5 fusion.7
  187.9 31.9 %copy.49 = bf16[4,192,4096]{1,0,2:T(4,128)(2,1)S(1)} copy(bf16[4,192,4096]{1,2,0:T(8,128)(2,1)S(1)} %fusion.7) | data formatting | bytes 12582912 | tf_op jit(solution)/shard_map/convert_element_type | solution.py:66
  219.8 190.2 %all_to_all.4 = bf16[4,192,4096]{1,0,2:T(4,128)(2,1)} all-to-all(bf16[4,192,4096]{1,0,2:T(4,128)(2,1)S(1)} %copy.49), channel_id=1, replica_groups=mesh['group'=2,'swap'=8,'image'=2] {'swap'}, dimensions={2} | all-to-all | bytes 12582912 | tf_op jit(solution)/shard_map/all_to_all | solution.py:67
  410.0 13.5 %copy.50 = bf16[4,192,4096]{2,1,0:T(8,128)(2,1)} copy(bf16[4,192,4096]{1,0,2:T(4,128)(2,1)} %all_to_all.4) | data formatting | bytes 12582912 | tf_op jit(solution)/shard_map/all_to_all | solution.py:67
  423.6 9.1 %copy.55 = f32[96,8,8,512]{3,2,1,0:T(8,128)S(1)} copy(bf16[96,8,8,512]{3,1,2,0:T(8,128)(2,1)} %bitcast.77) | data formatting | bytes 18874368
  432.6 1.0 fusion.19
  433.6 3.5 copy-done.1
  437.1 1.6 multiply_reduce_fusion
  438.7 10.6 %bitcast_bitcast_fusion = f32[4,8,192,512]{3,1,2,0:T(8,128)} fusion(f32[4,192,8,512]{3,2,1,0:T(8,128)} %bitcast.71), kind=kLoop, calls=%fused_computation.16 | loop fusion | bytes 25165824 | tf_op jit(solution)/shard_map/convert_element_type | solution.py:67
  449.4 16.7 %copy.51 = f32[4,8,192,512]{3,2,1,0:T(8,128)} copy(f32[4,8,192,512]{3,1,2,0:T(8,128)} %bitcast_bitcast_fusion) | data formatting | bytes 25165824 | tf_op jit(solution)/shard_map/convert_element_type | solution.py:67
  466.1 9.0 %fusion.15 = bf16[4,1536,512]{2,1,0:T(8,128)(2,1)} fusion(f32[4,8,192,512]{3,2,1,0:T(8,128)} %copy.51, f32[1536]{0:T(1024)S(1)} %copy-done.6, f32[1536]{0:T(1024)S(1)} %copy-done.7, f32[4,512]{1,0:T(4,128)S(1)} %add_rsqrt_fusion, f32[4,512]{1,0:T(4,128)S(1)} %broadcast_multiply_fusion), kind=kLoop, calls=%fused_computation.21 | loop fusion | flops 15728640 | bytes 18903040 | tf_op jit(solution)/shard_map/convert_element_type | solution.py:77
  475.1 8.7 %copy.52 = bf16[4,512,1536]{2,1,0:T(8,128)(2,1)} copy(bf16[4,512,1536]{1,2,0:T(8,128)(2,1)} %bitcast.78) | data formatting | bytes 12582912 | tf_op jit(solution)/shard_map/convert_element_type | solution.py:77
  483.8 0.0 all-gather.3.cloned.1.call-update
  483.8 0.0 all-gather.5.cloned.1.call-start
  483.9 0.1 copy.53
  484.0 0.7 mul.87
  484.7 1.6 fusion.18
  486.4 0.0 all-gather.5.cloned.1.call-update
  486.4 0.0 all-reduce.4.cloned.1.call-start
  486.4 21.3 %all-gather.3.cloned.1.call-done = bf16[4096,1536]{1,0:T(8,128)(2,1)} async-done(((bf16[2048,1536]{1,0:T(8,128)(2,1)}), bf16[4096,1536]{1,0:T(8,128)(2,1)}) %all-gather.3.cloned.1.call-update) | async-done | bytes 12582928 | tf_op jit(solution)/shard_map/all_gather | solution.py:79
  507.7 8.3 convolution_convert_fusion
  516.0 20.1 %fusion.20 = f32[4096,3072]{1,0:T(8,128)} fusion(bf16[4096,32]{0,1:T(8,128)(2,1)S(1)} %convolution_convert_fusion, bf16[32,3072]{1,0:T(8,128)(2,1)S(1)} %copy-done), kind=kOutput, calls=%fused_computation.33 | convolution fusion | flops 805306368 | bytes 50790400 | tf_op jit(solution)/shard_map/dot_general | solution.py:86
  536.2 112.2 %all-gather.5.cloned.1.call-done = bf16[1536,3072]{1,0:T(8,128)(2,1)} async-done(((bf16[192,3072]{1,0:T(8,128)(2,1)}), bf16[1536,3072]{1,0:T(8,128)(2,1)}) %all-gather.5.cloned.1.call-update) | async-done | bytes 9437200 | tf_op jit(solution)/shard_map/all_gather | solution.py:82
  648.3 64.7 %fusion.5 = bf16[4096,3072]{1,0:T(8,128)(2,1)} fusion(bf16[4096,3072]{1,0:T(8,128)(2,1)} %bitcast.80, f32[4096,3072]{1,0:T(8,128)} %fusion.20, bf16[4096,1536]{1,0:T(8,128)(2,1)} %all-gather.3.cloned.1.call-done, bf16[1536,3072]{1,0:T(8,128)(2,1)} %all-gather.5.cloned.1.call-done), kind=kOutput, calls=%fused_computation.6 | convolution fusion | flops 38818283520 | bytes 122683392 | tf_op jit(solution)/shard_map/dot_general | solution.py:84
  713.0 12.9 %fusion.21 = f32[4096,32]{0,1:T(8,128)} fusion(bf16[4096,3072]{1,0:T(8,128)(2,1)} %fusion.5, bf16[32,3072]{1,0:T(8,128)(2,1)S(1)} %copy-done), kind=kOutput, calls=%fused_computation.34 | convolution fusion | flops 805306368 | bytes 25886720 | tf_op jit(solution)/shard_map/dot_general | solution.py:92
  725.9 0.0 all-reduce.4.cloned.1.call-update
  725.9 0.0 all-reduce.6.cloned.1.call-start
  726.0 11.7 %convolution_multiply_fusion = f32[32,3072]{1,0:T(8,128)} fusion(bf16[4096,32]{0,1:T(8,128)(2,1)S(1)} %convolution_convert_fusion, bf16[4096,3072]{1,0:T(8,128)(2,1)} %fusion.5), kind=kOutput, calls=%fused_computation.25 | convolution fusion | flops 805404672 | bytes 25821184 | tf_op jit(solution)/shard_map/dot_general | solution.py:91
  737.7 5.2 all-reduce.4.cloned.1.call-done
  742.8 9.8 %convolution_multiply_fusion.1 = f32[1536,32]{0,1:T(8,128)} fusion(bf16[4096,1536]{1,0:T(8,128)(2,1)} %all-gather.3.cloned.1.call-done, f32[4096,32]{0,1:T(8,128)} %all-reduce.4.cloned.1.call-done), kind=kOutput, calls=%fused_computation.28 | convolution fusion | flops 2415968256 | bytes 13303808 | tf_op jit(solution)/shard_map/dot_general | solution.py:96
  752.6 0.0 all-reduce.6.cloned.1.call-update
  752.7 74.7 %all-reduce.6.cloned.1.call-done = (f32[1536,32]{0,1:T(8,128)}, f32[32,3072]{1,0:T(8,128)}) async-done(((f32[1536,32]{0,1:T(8,128)}, f32[32,3072]{1,0:T(8,128)}), (f32[1536,32]{0,1:T(8,128)}, f32[32,3072]{1,0:T(8,128)})) %all-reduce.6.cloned.1.call-update) | async-done | bytes 589840 | tf_op jit(solution)/shard_map/psum | solution.py:103
  827.3 1.6 copy.67
  829.0 1.8 copy.68
  (19 shorter events, 0.1 us)
Async XLA Ops:
  7.2 508.9 %copy-start = (bf16[32,3072]{1,0:T(8,128)(2,1)S(1)}, bf16[32,3072]{1,0:T(8,128)(2,1)}, u32[]{:S(2)}) copy-start(bf16[32,3072]{1,0:T(8,128)(2,1)} %param.18) | copy-start | bytes 589828
  7.2 500.5 %all-gather.3.cloned.1.call-start = ((), (), s32[]{:S(2)}) async-start(), calls=%async_computation.1 | async-start | bytes 18874368 | tf_op jit(solution)/shard_map/all_gather | solution.py:79
  40.2 5.3 copy-start.2
  45.5 4.2 copy-start.9
  167.4 17.9 %copy-start.8 = (f32[192]{0:T(256)S(1)}, f32[192]{0:T(256)}, u32[]{:S(2)}) copy-start(f32[192]{0:T(256)} %param.12) | copy-start | bytes 2308
  432.6 4.5 copy-start.1
  449.4 16.8 %copy-start.6 = (f32[1536]{0:T(1024)S(1)}, f32[1536]{0:T(1024)}, u32[]{:S(2)}) copy-start(f32[1536]{0:T(1024)} %param.14) | copy-start | bytes 18436
  449.4 16.8 %copy-start.7 = (f32[1536]{0:T(1024)S(1)}, f32[1536]{0:T(1024)}, u32[]{:S(2)}) copy-start(f32[1536]{0:T(1024)} %param.13) | copy-start | bytes 18436
  466.1 17.8 %copy-start.5 = (s32[192,24]{0,1:T(8,128)S(1)}, s32[192,24]{0,1:T(8,128)}, u32[]{:S(2)}) copy-start(s32[192,24]{0,1:T(8,128)} %param.16) | copy-start | bytes 55300
  466.1 18.6 %copy-start.3 = (bf16[192,3072]{1,0:T(8,128)(2,1)S(1)}, bf16[192,3072]{1,0:T(8,128)(2,1)}, u32[]{:S(2)}) copy-start(bf16[192,3072]{1,0:T(8,128)(2,1)} %param.15) | copy-start | bytes 3538948
  475.1 32.6 %copy-start.4 = (bf16[1536,32]{0,1:T(8,128)(2,1)S(1)}, bf16[1536,32]{0,1:T(8,128)(2,1)}, u32[]{:S(2)}) copy-start(bf16[1536,32]{0,1:T(8,128)(2,1)} %param.17) | copy-start | bytes 294916
  483.8 164.5 %all-gather.5.cloned.1.call-start = ((), (), s32[]{:S(2)}) async-start(), calls=%async_computation.2 | async-start | bytes 10616832 | tf_op jit(solution)/shard_map/all_gather | solution.py:82
  486.4 256.5 %all-reduce.4.cloned.1.call-start = ((), (), s32[]{:S(2)}) async-start(), calls=%async_computation.3 | async-start | bytes 1048576 | tf_op jit(solution)/shard_map/psum | solution.py:95
  725.9 101.4 %all-reduce.6.cloned.1.call-start = ((), (), s32[]{:S(2)}) async-start(), calls=%async_computation.4 | async-start | bytes 1179648 | tf_op jit(solution)/shard_map/psum | solution.py:103
Sparse Core Ops, SparseCore 0:
  484.0 23.7 all-gather.2
  509.9 138.3 all-gather.4
  726.0 16.7 all-reduce.3
  752.8 74.5 all-reduce.5
where the time goes:
time: 845 us; the launch traced here: 837 us
  matrix products  223 us (26%)
  waiting for transfers between devices  213 us (25%)
  blocking collectives  190 us (22%)
  local copies, waits for them, and re-layouts  176 us (21%)
  other arithmetic  20 us (2%)
  between operations  14.2 us (2%)
    all_to_all x1, blocking collectives, shards(): lax.all_to_all(conv, 'swap', split_axis=2, concat_axis=1, tiled=True)  190 us
    all_gather x1, waiting for transfers between devices, shards(): shard_rows = lax.all_gather(local_weight, 'swap', axis=0, tiled=True)  112 us
    conv_general_dilated x1, matrix products, depthwise(): lax.conv_general_dilated(maps, taps, (1, 1), ((half_span, half_span), (ha...  95.5 us
    psum x1, waiting for transfers between devices, shards(): grad_a, grad_b = lax.psum((grad_a_local, grad_b_local), 'swap')  74.7 us
    dot_general x1, matrix products, shards(): jnp.dot(columns, shard_rows, preferred_element_type=jnp.float32)  64.7 us
    conv_general_dilated x4, local copies, waits for them, and re-layouts, depthwise(): lax.conv_general_dilated(maps, taps, (1, 1), ((half_span, half_span), (ha...  43.4 us
    unnamed x25, local copies, waits for them, and re-layouts  40 us
    convert_element_type x1, local copies, waits for them, and re-layouts, shards(): conv = depthwise(images_in, kernel, conv_bias, W).astype(jnp.bfloat16)  31.9 us
  transfers between devices with their start and end apart: 4, of which 4 were waited for; matrix products, arithmetic and copies ran while one was open for 5% of the time, Pallas kernels for 0%

commit v1 on v0

--- a/solution.py
+++ b/solution.py
@@ -7,6 +7,27 @@
 W = 64
 adapter_scale = 2.0
 norm_eps = 1e-06
+
+
+def ring_gather(shard, axis, dim):
+    devices, position, width = (lax.axis_size(axis), lax.axis_index(axis), shard.shape[dim])
+    right = [(i, (i + 1) % devices) for i in range(devices)]
+    backward = [(i, (i - 1) % devices) for i in range(devices)]
+    result = jnp.zeros((*shard.shape[:dim], devices * width, *shard.shape[dim + 1 :]), shard.dtype)
+    result = lax.dynamic_update_slice_in_dim(result, shard, position * width, axis=dim)
+    from_left = from_right = shard
+    middle = devices // 2
+    for step in range(1, middle + 1):
+        from_left = lax.ppermute(from_left, axis, right)
+        result = lax.dynamic_update_slice_in_dim(
+            result, from_left, (position - step) % devices * width, axis=dim
+        )
+        if step < devices - middle:
+            from_right = lax.ppermute(from_right, axis, backward)
+            result = lax.dynamic_update_slice_in_dim(
+                result, from_right, (position + step) % devices * width, axis=dim
+            )
+    return result
 
 
 def power_table(scales):
@@ -79,7 +100,7 @@
     tokens = lax.all_gather(own_rows, "image", axis=0, tiled=True)
     zero_start = jnp.zeros((tokens.shape[0], fp8_weight.shape[1]), jnp.float32)
     local_weight = decode(fp8_weight, block_scale)
-    shard_rows = lax.all_gather(local_weight, "swap", axis=0, tiled=True)
+    shard_rows = ring_gather(local_weight, "swap", 0)
     columns = lax.slice_in_dim(tokens, 0, shard_rows.shape[0], axis=1)
     frozen = zero_start + jnp.dot(columns, shard_rows, preferred_element_type=jnp.float32)
     low_rank = jnp.dot(tokens, adapter_a, preferred_element_type=jnp.float32).astype(jnp.bfloat16)

time: 845 us -> 898 us (1.063)
  waiting for transfers between devices: 213 us -> 235 us
  local copies, waits for them, and re-layouts: 176 us -> 193 us
  starting transfers between devices: 0.16 us -> 17 us
    ppermute x0 -> x7, waiting for transfers between devices: none -> 156 us  [the longest x4 156 us: ring_gather(): from_left = lax.ppermute(from_left, axis, right)]
    all_gather x1 -> x0, waiting for transfers between devices: 112 us -> none  [shards(): shard_rows = lax.all_gather(local_weight, 'swap', axis=0, tiled=True)]
    all_gather x1, waiting for transfers between devices: 21.3 us -> 0.01 us  [shards(): tokens = lax.all_gather(own_rows, 'image', axis=0, tiled=True)]
    ppermute x0 -> x7, starting transfers between devices: none -> 16.7 us  [the longest x4 8.72 us: ring_gather(): from_left = lax.ppermute(from_left, axis, right)]
    dynamic_update_slice x0 -> x7, local copies, waits for them, and re-layouts: none -> 11.7 us  [the longest x4 7.08 us: ring_gather(): lax.dynamic_update_slice_in_dim(result, from_left, (position - step) % de...]
    unnamed x25 -> x29, local copies, waits for them, and re-layouts: 40 us -> 43.4 us
  transfers between devices with their start and end apart: 4 -> 10, of which waited for: 4 -> 6; matrix products, arithmetic and copies ran while one was open for 5% -> 3% of each run, Pallas kernels for 0% -> 0%
where the time goes in v1:
time: 898 us; the launch traced here: 890 us
  waiting for transfers between devices  235 us (26%)
  matrix products  222 us (25%)
  local copies, waits for them, and re-layouts  193 us (21%)
  blocking collectives  190 us (21%)
  other arithmetic  19 us (2%)
  starting transfers between devices  17 us (2%)
  between operations  14.2 us (2%)
    all_to_all x1, blocking collectives, shards(): lax.all_to_all(conv, 'swap', split_axis=2, concat_axis=1, tiled=True)  190 us
    ppermute x4, waiting for transfers between devices, ring_gather(): from_left = lax.ppermute(from_left, axis, right)  156 us
    conv_general_dilated x1, matrix products, depthwise(): lax.conv_general_dilated(maps, taps, (1, 1), ((half_span, half_span), (ha...  95.5 us
    psum x1, waiting for transfers between devices, shards(): grad_a, grad_b = lax.psum((grad_a_local, grad_b_local), 'swap')  74.7 us
    dot_general x1, matrix products, shards(): jnp.dot(columns, shard_rows, preferred_element_type=jnp.float32)  64.8 us
    unnamed x29, local copies, waits for them, and re-layouts  43.4 us
    conv_general_dilated x4, local copies, waits for them, and re-layouts, depthwise(): lax.conv_general_dilated(maps, taps, (1, 1), ((half_span, half_span), (ha...  43.4 us
    convert_element_type x1, local copies, waits for them, and re-layouts, shards(): conv = depthwise(images_in, kernel, conv_bias, W).astype(jnp.bfloat16)  31.9 us
  transfers between devices with their start and end apart: 10, of which 6 were waited for; matrix products, arithmetic and copies ran while one was open for 3% of the time, Pallas kernels for 0%

profile of v1, /device:TPU:0, one launch (start us, length us, event | category | flops | bytes accessed | tf_op | source)
XLA Modules:
  0.0 890.4 jit_solution(12223512320984296877)
XLA Ops:
  8.1 10.7 %copy.43 = bf16[4,192,4096]{1,2,0:T(8,128)(2,1)} copy(bf16[4,192,4096]{2,1,0:T(8,128)(2,1)} %param.10) | data formatting | bytes 12582912 | tf_op args[0]
  18.7 11.6 %copy.54 = bf16[192,64,4,64]{0,1,3,2:T(8,128)(2,1)} copy(bf16[192,64,4,64]{0,3,1,2:T(8,128)(2,1)} %bitcast.76) | data formatting | bytes 12582912
  30.3 10.0 %pad.clone = bf16[192,64,4,72]{0,1,3,2:T(8,128)(2,1)} pad(bf16[192,64,4,64]{0,1,3,2:T(8,128)(2,1)} %copy.54, bf16[]{:T(256)} %constant.48.clone.1), padding=0_0x0_0x0_0x3_5 | pad | bytes 13369346 | tf_op jit(solution)/shard_map/reshape | solution.py:59
  40.3 3.4 slice.2
  43.7 1.9 copy-done.2
  45.6 4.2 fusion.8
  49.8 95.5 %broadcast_select_fusion = f32[64,32,9,192]{3,1,2,0:T(8,128)S(1)} fusion(pred[32,9]{0,1:T(8,128)(4,1)S(1)} %copy-done.11, bf16[192,1,7,7]{0,1,3,2:T(2,128)(2,1)S(1)} %reshape.62, bf16[192,64,4,8,15]{0,1,4,3,2:T(8,128)(2,1)S(1)} %fusion.8), kind=kOutput, calls=%fused_computation.23 | convolution fusion | flops 341065728 | bytes 25971360 | tf_op jit(solution)/shard_map/conv_general_dilated | solution.py:62
  145.3 20.1 %copy.47 = f32[64,32,9,192]{3,0,2,1:T(8,128)S(1)} copy(f32[64,32,9,192]{3,1,2,0:T(8,128)S(1)} %broadcast_select_fusion) | data formatting | bytes 28311552 | tf_op jit(solution)/shard_map/conv_general_dilated | solution.py:62
  165.4 2.0 slice_bitcast_fusion
  167.5 17.9 %copy.48 = f32[4,192,64,64]{1,3,2,0:T(8,128)S(1)} copy(f32[4,192,64,64]{1,2,3,0:T(8,128)S(1)} %slice_bitcast_fusion) | data formatting | bytes 25165824 | tf_op jit(solution)/shard_map/conv_general_dilated | solution.py:62
  185.4 2.5 fusion.7
  188.0 31.9 %copy.49 = bf16[4,192,4096]{1,0,2:T(4,128)(2,1)S(1)} copy(bf16[4,192,4096]{1,2,0:T(8,128)(2,1)S(1)} %fusion.7) | data formatting | bytes 12582912 | tf_op jit(solution)/shard_map/convert_element_type | solution.py:87
  219.8 190.2 %all_to_all.4 = bf16[4,192,4096]{1,0,2:T(4,128)(2,1)} all-to-all(bf16[4,192,4096]{1,0,2:T(4,128)(2,1)S(1)} %copy.49), channel_id=1, replica_groups=mesh['group'=2,'swap'=8,'image'=2] {'swap'}, dimensions={2} | all-to-all | bytes 12582912 | tf_op jit(solution)/shard_map/all_to_all | solution.py:88
  410.1 13.5 %copy.50 = bf16[4,192,4096]{2,1,0:T(8,128)(2,1)} copy(bf16[4,192,4096]{1,0,2:T(4,128)(2,1)} %all_to_all.4) | data formatting | bytes 12582912 | tf_op jit(solution)/shard_map/all_to_all | solution.py:88
  423.6 9.1 %copy.55 = f32[96,8,8,512]{3,2,1,0:T(8,128)S(1)} copy(bf16[96,8,8,512]{3,1,2,0:T(8,128)(2,1)} %bitcast.78) | data formatting | bytes 18874368
  433.7 1.7 multiply_reduce_fusion
  435.4 2.4 copy-done.1
  437.8 10.6 %bitcast_bitcast_fusion = f32[4,8,192,512]{3,1,2,0:T(8,128)} fusion(f32[4,192,8,512]{3,2,1,0:T(8,128)} %bitcast.72), kind=kLoop, calls=%fused_computation.16 | loop fusion | bytes 25165824 | tf_op jit(solution)/shard_map/convert_element_type | solution.py:88
  448.4 16.8 %copy.51 = f32[4,8,192,512]{3,2,1,0:T(8,128)} copy(f32[4,8,192,512]{3,1,2,0:T(8,128)} %bitcast_bitcast_fusion) | data formatting | bytes 25165824 | tf_op jit(solution)/shard_map/convert_element_type | solution.py:88
  465.2 8.9 fusion.15
  474.0 8.8 copy.52
  483.7 1.2 broadcast_in_dim.77
  485.6 4.4 copy-done.3
  491.2 3.6 collective-permute-start.1
  494.8 45.4 %collective-permute-done = bf16[192,3072]{1,0:T(8,128)(2,1)S(1)} collective-permute-done((bf16[192,3072]{1,0:T(8,128)(2,1)S(1)}, bf16[192,3072]{1,0:T(8,128)(2,1)S(1)}, u32[]{:S(2)}, u32[]{:S(2)}) %collective-permute-start) | collective-permute-done | bytes 1179680 | tf_op jit(solution)/shard_map/ppermute | solution.py:21
  540.2 2.5 collective-permute-start.2
  542.7 2.2 collective-permute-start.3
  544.9 47.1 %collective-permute-done.2 = bf16[192,3072]{1,0:T(8,128)(2,1)} collective-permute-done((bf16[192,3072]{1,0:T(8,128)(2,1)S(1)}, bf16[192,3072]{1,0:T(8,128)(2,1)}, u32[]{:S(2)}, u32[]{:S(2)}) %collective-permute-start.2) | collective-permute-done | bytes 1179680 | tf_op jit(solution)/shard_map/ppermute | solution.py:21
  592.0 2.6 collective-permute-start.4
  594.5 2.4 constant_dynamic-update-slice_fusion.6
  597.0 2.1 collective-permute-start.5
  599.1 2.3 constant_dynamic-update-slice_fusion.5
  601.5 42.9 %collective-permute-done.4 = bf16[192,3072]{1,0:T(8,128)(2,1)S(1)} collective-permute-done((bf16[192,3072]{1,0:T(8,128)(2,1)}, bf16[192,3072]{1,0:T(8,128)(2,1)S(1)}, u32[]{:S(2)}, u32[]{:S(2)}) %collective-permute-start.4) | collective-permute-done | bytes 1179680 | tf_op jit(solution)/shard_map/ppermute | solution.py:21
  644.4 2.5 collective-permute-start.6
  646.9 2.4 constant_dynamic-update-slice_fusion.4
  649.3 1.1 constant_dynamic-update-slice_fusion.3
  651.6 1.2 constant_dynamic-update-slice_fusion.1
  652.7 20.4 %collective-permute-done.6 = bf16[192,3072]{1,0:T(8,128)(2,1)S(1)} collective-permute-done((bf16[192,3072]{1,0:T(8,128)(2,1)S(1)}, bf16[192,3072]{1,0:T(8,128)(2,1)S(1)}, u32[]{:S(2)}, u32[]{:S(2)}) %collective-permute-start.6) | collective-permute-done | bytes 1179680 | tf_op jit(solution)/shard_map/ppermute | solution.py:21
  674.2 8.3 convolution_convert_fusion
  682.5 19.4 %fusion.21 = f32[4096,3072]{1,0:T(8,128)} fusion(bf16[4096,32]{0,1:T(8,128)(2,1)S(1)} %convolution_convert_fusion, bf16[32,3072]{1,0:T(8,128)(2,1)S(1)} %copy-done), kind=kOutput, calls=%fused_computation.41 | convolution fusion | flops 805306368 | bytes 50790400 | tf_op jit(solution)/shard_map/dot_general | solution.py:107
  701.9 64.8 %fusion.5 = bf16[4096,3072]{1,0:T(8,128)(2,1)} fusion(bf16[4096,3072]{1,0:T(8,128)(2,1)} %bitcast.81, f32[4096,3072]{1,0:T(8,128)} %fusion.21, bf16[4096,1536]{1,0:T(8,128)(2,1)} %all-gather.2.cloned.1.call-done, bf16[1536,3072]{1,0:T(8,128)(2,1)} %constant_dynamic-update-slice_fusion), kind=kOutput, calls=%fused_computation.6 | convolution fusion | flops 38818283520 | bytes 122683392 | tf_op jit(solution)/shard_map/dot_general | solution.py:105
  766.7 12.9 %fusion.22 = f32[4096,32]{0,1:T(8,128)} fusion(bf16[4096,3072]{1,0:T(8,128)(2,1)} %fusion.5, bf16[32,3072]{1,0:T(8,128)(2,1)S(1)} %copy-done), kind=kOutput, calls=%fused_computation.42 | convolution fusion | flops 805306368 | bytes 25886720 | tf_op jit(solution)/shard_map/dot_general | solution.py:113
  779.9 11.5 %convolution_multiply_fusion = f32[32,3072]{1,0:T(8,128)} fusion(bf16[4096,32]{0,1:T(8,128)(2,1)S(1)} %convolution_convert_fusion, bf16[4096,3072]{1,0:T(8,128)(2,1)} %fusion.5), kind=kOutput, calls=%fused_computation.25 | convolution fusion | flops 805404672 | bytes 25821184 | tf_op jit(solution)/shard_map/dot_general | solution.py:112
  791.4 4.3 all-reduce.4.cloned.1.call-done
  795.6 9.9 %convolution_multiply_fusion.1 = f32[1536,32]{0,1:T(8,128)} fusion(bf16[4096,1536]{1,0:T(8,128)(2,1)} %all-gather.2.cloned.1.call-done, f32[4096,32]{0,1:T(8,128)} %all-reduce.4.cloned.1.call-done), kind=kOutput, calls=%fused_computation.28 | convolution fusion | flops 2415968256 | bytes 13303808 | tf_op jit(solution)/shard_map/dot_general | solution.py:117
  805.6 74.7 %all-reduce.6.cloned.1.call-done = (f32[1536,32]{0,1:T(8,128)}, f32[32,3072]{1,0:T(8,128)}) async-done(((f32[1536,32]{0,1:T(8,128)}, f32[32,3072]{1,0:T(8,128)}), (f32[1536,32]{0,1:T(8,128)}, f32[32,3072]{1,0:T(8,128)})) %all-reduce.6.cloned.1.call-update) | async-done | bytes 589840 | tf_op jit(solution)/shard_map/psum | solution.py:124
  880.3 1.6 copy.76
  881.9 1.8 copy.77
  (42 shorter events, 7.1 us)
Async XLA Ops:
  7.2 675.3 %copy-start = (bf16[32,3072]{1,0:T(8,128)(2,1)S(1)}, bf16[32,3072]{1,0:T(8,128)(2,1)}, u32[]{:S(2)}) copy-start(bf16[32,3072]{1,0:T(8,128)(2,1)} %param.18) | copy-start | bytes 589828
  7.2 667.0 %all-gather.2.cloned.1.call-start = ((), (), s32[]{:S(2)}) async-start(), calls=%async_computation.1 | async-start | bytes 18874368 | tf_op jit(solution)/shard_map/all_gather | solution.py:100
  40.3 5.3 copy-start.2
  45.6 4.2 copy-start.11
  167.4 17.9 %copy-start.10 = (f32[192]{0:T(256)S(1)}, f32[192]{0:T(256)}, u32[]{:S(2)}) copy-start(f32[192]{0:T(256)} %param.12) | copy-start | bytes 2308
  432.7 5.1 copy-start.1
  448.4 16.8 %copy-start.8 = (f32[1536]{0:T(1024)S(1)}, f32[1536]{0:T(1024)}, u32[]{:S(2)}) copy-start(f32[1536]{0:T(1024)} %param.14) | copy-start | bytes 18436
  448.4 16.8 %copy-start.9 = (f32[1536]{0:T(1024)S(1)}, f32[1536]{0:T(1024)}, u32[]{:S(2)}) copy-start(f32[1536]{0:T(1024)} %param.13) | copy-start | bytes 18436
  474.0 8.8 copy-start.7
  474.0 10.9 %copy-start.5 = (bf16[192,3072]{1,0:T(8,128)(2,1)S(1)}, bf16[192,3072]{1,0:T(8,128)(2,1)}, u32[]{:S(2)}) copy-start(bf16[192,3072]{1,0:T(8,128)(2,1)} %param.15) | copy-start | bytes 3538948
  482.8 312.8 %all-reduce.4.cloned.1.call-start = ((), (), s32[]{:S(2)}) async-start(), calls=%async_computation.2 | async-start | bytes 1048576 | tf_op jit(solution)/shard_map/psum | solution.py:116
  484.9 189.3 %copy-start.6 = (bf16[1536,32]{0,1:T(8,128)(2,1)S(1)}, bf16[1536,32]{0,1:T(8,128)(2,1)}, u32[]{:S(2)}) copy-start(bf16[1536,32]{0,1:T(8,128)(2,1)} %param.17) | copy-start | bytes 294916
  485.6 4.4 copy-start.3
  490.1 50.1 %collective-permute-start = (bf16[192,3072]{1,0:T(8,128)(2,1)S(1)}, bf16[192,3072]{1,0:T(8,128)(2,1)S(1)}, u32[]{:S(2)}, u32[]{:S(2)}) collective-permute-start(bf16[192,3072]{1,0:T(8,128)(2,1)S(1)} %get-tuple-element.5), channel_id=1, source_target_pairs={{0,2},{2,4},{4,6},{6,8},{8,10},{10,12},{12,14},{14,0},{1,3},{3,5},... | collective-permute-start | bytes 3538952 | tf_op jit(solution)/shard_map/ppermute | solution.py:21
  491.2 51.5 %collective-permute-start.1 = (bf16[192,3072]{1,0:T(8,128)(2,1)S(1)}, bf16[192,3072]{1,0:T(8,128)(2,1)}, u32[]{:S(2)}, u32[]{:S(2)}) collective-permute-start(bf16[192,3072]{1,0:T(8,128)(2,1)S(1)} %get-tuple-element.5), channel_id=1, source_target_pairs={{0,14},{2,0},{4,2},{6,4},{8,6},{10,8},{12,10},{14,12},{1,15},{3,1}... | collective-permute-start | bytes 3538952 | tf_op jit(solution)/shard_map/ppermute | solution.py:26
  540.2 4.7 copy-start.4
  540.2 51.8 %collective-permute-start.2 = (bf16[192,3072]{1,0:T(8,128)(2,1)S(1)}, bf16[192,3072]{1,0:T(8,128)(2,1)}, u32[]{:S(2)}, u32[]{:S(2)}) collective-permute-start(bf16[192,3072]{1,0:T(8,128)(2,1)S(1)} %collective-permute-done), channel_id=1, source_target_pairs={{0,2},{2,4},{4,6},{6,8},{8,10},{10,12},{12,14},{14,0},{1,3},{3,5},... | collective-permute-start | bytes 3538952 | tf_op jit(solution)/shard_map/ppermute | solution.py:21
  542.7 54.3 %collective-permute-start.3 = (bf16[192,3072]{1,0:T(8,128)(2,1)}, bf16[192,3072]{1,0:T(8,128)(2,1)S(1)}, u32[]{:S(2)}, u32[]{:S(2)}) collective-permute-start(bf16[192,3072]{1,0:T(8,128)(2,1)} %collective-permute-done.1), channel_id=1, source_target_pairs={{0,14},{2,0},{4,2},{6,4},{8,6},{10,8},{12,10},{14,12},{1,15},{3,1}... | collective-permute-start | bytes 3538952 | tf_op jit(solution)/shard_map/ppermute | solution.py:26
  592.0 52.4 %collective-permute-start.4 = (bf16[192,3072]{1,0:T(8,128)(2,1)}, bf16[192,3072]{1,0:T(8,128)(2,1)S(1)}, u32[]{:S(2)}, u32[]{:S(2)}) collective-permute-start(bf16[192,3072]{1,0:T(8,128)(2,1)} %collective-permute-done.2), channel_id=1, source_target_pairs={{0,2},{2,4},{4,6},{6,8},{8,10},{10,12},{12,14},{14,0},{1,3},{3,5},... | collective-permute-start | bytes 3538952 | tf_op jit(solution)/shard_map/ppermute | solution.py:21
  597.0 54.6 %collective-permute-start.5 = (bf16[192,3072]{1,0:T(8,128)(2,1)S(1)}, bf16[192,3072]{1,0:T(8,128)(2,1)S(1)}, u32[]{:S(2)}, u32[]{:S(2)}) collective-permute-start(bf16[192,3072]{1,0:T(8,128)(2,1)S(1)} %collective-permute-done.3), channel_id=1, source_target_pairs={{0,14},{2,0},{4,2},{6,4},{8,6},{10,8},{12,10},{14,12},{1,15},{3,1}... | collective-permute-start | bytes 3538952 | tf_op jit(solution)/shard_map/ppermute | solution.py:26
  644.4 28.7 %collective-permute-start.6 = (bf16[192,3072]{1,0:T(8,128)(2,1)S(1)}, bf16[192,3072]{1,0:T(8,128)(2,1)S(1)}, u32[]{:S(2)}, u32[]{:S(2)}) collective-permute-start(bf16[192,3072]{1,0:T(8,128)(2,1)S(1)} %collective-permute-done.4), channel_id=1, source_target_pairs={{0,2},{2,4},{4,6},{6,8},{8,10},{10,12},{12,14},{14,0},{1,3},{3,5},... | collective-permute-start | bytes 3538952 | tf_op jit(solution)/shard_map/ppermute | solution.py:21
  779.6 100.7 %all-reduce.6.cloned.1.call-start = ((), (), s32[]{:S(2)}) async-start(), calls=%async_computation.3 | async-start | bytes 1179648 | tf_op jit(solution)/shard_map/psum | solution.py:124
Sparse Core Ops, SparseCore 0:
  483.0 23.7 all-gather.1
  779.7 15.8 all-reduce.3
  805.7 74.5 all-reduce.5
